TPU v7x, 32 devices: a whole 2x2x4 slice. The times are simulated.
32 devices in a mesh: expert: 16 (over z, x, core), tensor: 2 (over y).
Axes of the slice: x: 2, y: 2, z: 4, core: 2. Of those that a mesh axis runs over, the one named last changes fastest.
Arguments:
- tokens: bfloat16 [256, 7168], P('expert', 'tensor'), may hold values from -6 to 6
- expert_ids: int32 [256, 8], P('expert'), may hold values from 0 to 7, as said below
- route_weights: float32 [256, 8], P('expert'), may hold values from 0.05 to 1
- gate_weight: bfloat16 [16, 512, 7168], P('expert', 'tensor'), may hold values from -0.0625 to 0.0625
- up_weight: bfloat16 [16, 512, 7168], P('expert', 'tensor'), may hold values from -0.0625 to 0.0625
- down_weight: bfloat16 [16, 512, 7168], P('expert', 'tensor'), may hold values from -0.1875 to 0.1875
Outputs:
- mixed: bfloat16 [256, 7168], P('expert', 'tensor')
Inputs may be any that keep to these rules, and one draw needn't show every extreme that they name: `expert_ids`: each row holds 8 different experts. One expert, the same for all tokens, is named by exactly 16 of the 16 tokens of every block of 16 consecutive tokens; every other expert by at most 16 tokens of a block.
All inputs are finite; a program needn't handle non-finite values.
Results may differ from a plain program's by a relative error of at most 0.015.
Values may be sent and summed in bfloat16 or wider, within the bound.
A program may use at most 64 MiB of HBM per device.

v0:
```python
import jax
import jax.numpy as jnp
from jax import lax
from jax.sharding import PartitionSpec as P


def rows_times(rows, weight):
    return lax.dot_general(
        rows, weight, (((1,), (1,)), ((), ())), preferred_element_type=jnp.float32
    )


def body(tokens, expert_ids, route_weights, gate_weight, up_weight, down_weight):
    devices_wide = lax.axis_size("expert")
    experts = devices_wide // 2
    tok_count = expert_ids.shape[0]
    per_token = expert_ids.shape[1]
    capacity = min(tok_count, tok_count * per_token // experts)
    slot_count = experts * capacity
    arrived_count = devices_wide * capacity
    expert_range = jnp.arange(experts, dtype=jnp.int32)
    onehot = jnp.sum(
        (expert_ids[:, :, None] == expert_range[None, None, :]).astype(jnp.int32), axis=1
    )
    earlier_count = jnp.cumsum(onehot, axis=0) - onehot
    slot_rank = jnp.take_along_axis(earlier_count, expert_ids, axis=1)
    slot_of = expert_ids * capacity + slot_rank
    slot_range = jnp.arange(slot_count, dtype=jnp.int32)
    select = jnp.any(slot_of[None, :, :] == slot_range[:, None, None], axis=2).astype(jnp.bfloat16)
    weight_gate = gate_weight[0]
    weight_up = up_weight[0]
    weight_out = down_weight[0]
    whole_rows = lax.all_gather(tokens, "tensor", axis=1, tiled=True)
    packed = jnp.dot(select, whole_rows, preferred_element_type=jnp.float32).astype(jnp.bfloat16)
    packed = packed.reshape(experts, capacity, whole_rows.shape[1])
    arrived = lax.all_to_all(
        jnp.repeat(packed, 2, axis=0), "expert", split_axis=0, concat_axis=0, tiled=True
    ).reshape(arrived_count, -1)
    gate_act = rows_times(arrived, weight_gate)
    up_act = rows_times(arrived, weight_up)
    hidden = (jax.nn.silu(gate_act) * up_act).astype(jnp.bfloat16)
    columns = lax.all_to_all(weight_out, "tensor", split_axis=1, concat_axis=0, tiled=True)
    unit_count = hidden.shape[1]
    shard_piece = lax.all_gather(hidden, "tensor", axis=1, tiled=True)
    groups = shard_piece.shape[1] // unit_count
    weight_rows = columns
    weight_rows = weight_rows.reshape(groups, unit_count, columns.shape[1])
    grouped = shard_piece.reshape(shard_piece.shape[0], groups, unit_count)
    group_terms = jnp.einsum(
        "rgf,gfd->grd", grouped, weight_rows, preferred_element_type=jnp.float32
    ).astype(jnp.bfloat16)
    group_terms = lax.optimization_barrier(group_terms)
    half_out = jnp.sum(group_terms.astype(jnp.float32), axis=0).astype(jnp.bfloat16)
    returned = lax.all_to_all(
        half_out.reshape(devices_wide, capacity, -1),
        "expert",
        split_axis=0,
        concat_axis=0,
        tiled=True,
    )
    returned = returned.reshape(experts, 2, capacity, -1).astype(jnp.float32)
    combined = (returned[:, 0] + returned[:, 1]).reshape(slot_count, -1)
    picked = combined[slot_of]
    mixed_out = jnp.sum(route_weights[:, :, None] * picked, axis=1)
    return mixed_out.astype(jnp.bfloat16)


def solution(mesh):
    placed = (
        P("expert", "tensor"),
        P("expert", None),
        P("expert", None),
        P("expert", "tensor", None),
        P("expert", "tensor", None),
        P("expert", "tensor", None),
    )
    return jax.shard_map(
        body, mesh=mesh, in_specs=placed, out_specs=P("expert", "tensor"), check_vma=False
    )
```

profile of v0, /device:TPU:11, one launch (start us, length us, event | category | flops | bytes accessed | tf_op | source)
XLA Modules:
  0.0 212.2 jit_solution(18340728612617636076)
XLA Ops:
  0.0 0.7 convert_reduce_fusion
  0.7 0.7 bitcast_or_fusion
  1.4 0.1 copy.24
  1.5 0.1 copy.26
  1.6 0.1 reshape.55
  1.7 0.0 copy-start.1
  1.7 0.0 copy-start
  1.7 1.3 gather_fusion.1
  3.0 0.1 reshape.58
  3.1 0.1 copy.27
  3.1 0.0 copy-done.1
  3.2 0.1 copy.28
  3.2 0.1 fusion.14
  3.3 0.0 copy-done
  3.3 4.7 %all_gather.6 = bf16[16,7168]{1,0:T(8,128)(2,1)S(1)} all-gather(bf16[16,3584]{1,0:T(8,128)(2,1)S(1)} %copy-done), channel_id=1, replica_groups=mesh['expert'=16,'tensor'=2] {'tensor'}, dimensions={1}, use_global_device_ids=true | all-gather | bytes 344064 | tf_op jit(solution)/shard_map/all_gather | solution.py:33
  8.0 0.7 convolution_convert_fusion
  8.7 2.3 %broadcast_in_dim.16 = bf16[8,2,16,7168]{3,2,1,0:T(8,128)(2,1)} broadcast(bf16[8,16,7168]{2,1,0:T(8,128)(2,1)S(1)} %bitcast.41), dimensions={0,2,3} | broadcast | bytes 5505024 | tf_op jit(solution)/shard_map/broadcast_in_dim | solution.py:37
  11.1 7.4 %all-to-all-start = ((bf16[16,16,7168]{2,1,0:T(8,128)(2,1)}), bf16[16,16,7168]{2,1,0:T(8,128)(2,1)}, u32[]{:S(2)}, u32[]{:S(2)}) async-start(bf16[16,16,7168]{2,1,0:T(8,128)(2,1)} %bitcast.39), calls=%async_computation | async-start | bytes 7340032 | tf_op jit(solution)/shard_map/all_to_all | solution.py:36
  18.4 5.9 %copy.29 = bf16[1,256,7168]{1,2,0:T(8,128)(2,1)} copy(bf16[1,256,7168]{2,1,0:T(8,128)(2,1)} %param.11) | data formatting | bytes 7340032 | tf_op args[5]
  24.4 6.0 %copy.30 = bf16[256,2,3584]{2,0,1:T(8,128)(2,1)} copy(bf16[256,2,3584]{0,2,1:T(8,128)(2,1)} %bitcast.38) | data formatting | bytes 7340032 | tf_op jit(solution)/shard_map/all_to_all | solution.py:42
  30.3 69.4 %all-to-all-done = bf16[16,16,7168]{2,1,0:T(8,128)(2,1)} async-done(((bf16[16,16,7168]{2,1,0:T(8,128)(2,1)}), bf16[16,16,7168]{2,1,0:T(8,128)(2,1)}, u32[]{:S(2)}, u32[]{:S(2)}) %all-to-all-start) | async-done | bytes 3670048 | tf_op jit(solution)/shard_map/all_to_all | solution.py:36
  99.7 5.5 %all-to-all-start.1 = ((bf16[256,2,3584]{2,0,1:T(8,128)(2,1)}), bf16[256,2,3584]{2,0,1:T(8,128)(2,1)}, u32[]{:S(2)}, u32[]{:S(2)}) async-start(bf16[256,2,3584]{2,0,1:T(8,128)(2,1)} %copy.30), calls=%async_computation.1 | async-start | bytes 7340032 | tf_op jit(solution)/shard_map/all_to_all | solution.py:42
  105.2 0.0 copy-start.3
  105.2 4.4 %fusion.3 = f32[256,256]{1,0:T(8,128)S(1)} fusion(bf16[256,7168]{1,0:T(8,128)(2,1)} %bitcast.3, bf16[1,256,7168]{2,1,0:T(8,128)(2,1)} %param.9), kind=kOutput, calls=%fused_computation.7 | convolution fusion | flops 939524096 | bytes 7602176 | tf_op jit(solution)/shard_map/dot_general | solution.py:8
  109.6 0.0 copy-done.3
  109.6 3.2 %fusion.9 = bf16[256,256]{1,0:T(8,128)(2,1)S(1)} fusion(bf16[256,7168]{1,0:T(8,128)(2,1)} %bitcast.3, bf16[1,256,7168]{2,1,0:T(8,128)(2,1)S(1)} %copy-done.3, f32[256,256]{1,0:T(8,128)S(1)} %fusion.3), kind=kOutput, calls=%fused_computation.13 | convolution fusion | flops 939917312 | bytes 7733248 | tf_op jit(solution)/shard_map/dot_general | solution.py:8
  112.8 36.8 %all_gather.7 = bf16[256,512]{1,0:T(8,128)(2,1)S(1)} all-gather(bf16[256,256]{1,0:T(8,128)(2,1)S(1)} %fusion.9), channel_id=1, replica_groups=mesh['expert'=16,'tensor'=2] {'tensor'}, dimensions={1}, use_global_device_ids=true | all-gather | bytes 393216 | tf_op jit(solution)/shard_map/all_gather | solution.py:44
  149.6 0.0 all-to-all-done.1
  149.6 5.0 %convolution_convert_fusion.1 = bf16[2,256,3584]{2,1,0:T(8,128)(2,1)} fusion(bf16[256,2,3584]{2,0,1:T(8,128)(2,1)} %all-to-all-done.1, bf16[32,2,8,256]{3,2,1,0:T(8,128)(2,1)S(1)} %bitcast.42), kind=kOutput, calls=%fused_computation.3 | convolution fusion | flops 941359104 | bytes 7602176 | tf_op jit(solution)/shard_map/rgf,gfd->grd/dot_general | solution.py:49
  154.6 0.0 copy-start.2
  154.6 4.4 %reduce_sum.31 = bf16[256,3584]{1,0:T(8,128)(2,1)} reduce(bf16[2,256,3584]{2,1,0:T(8,128)(2,1)} %convolution_convert_fusion.1, bf16[]{:T(256)} %constant.31.clone.1), dimensions={0}, to_apply=%region_3.4 | reduce | flops 917504 | bytes 5505026 | tf_op jit(solution)/shard_map/reduce_sum | solution.py:53
  159.0 5.6 %all-to-all-start.2 = ((bf16[16,16,3584]{2,1,0:T(8,128)(2,1)}), bf16[16,16,3584]{2,1,0:T(8,128)(2,1)S(1)}, u32[]{:S(2)}, u32[]{:S(2)}) async-start(bf16[16,16,3584]{2,1,0:T(8,128)(2,1)} %bitcast.8), calls=%async_computation.2 | async-start | bytes 3670016 | tf_op jit(solution)/shard_map/all_to_all | solution.py:54
  164.6 0.1 copy.32
  164.7 0.1 reshape.49
  164.8 0.0 copy-done.2
  164.8 0.1 copy.23
  164.9 41.6 %all-to-all-done.2 = bf16[16,16,3584]{2,1,0:T(8,128)(2,1)S(1)} async-done(((bf16[16,16,3584]{2,1,0:T(8,128)(2,1)}), bf16[16,16,3584]{2,1,0:T(8,128)(2,1)S(1)}, u32[]{:S(2)}, u32[]{:S(2)}) %all-to-all-start.2) | async-done | bytes 1835040 | tf_op jit(solution)/shard_map/all_to_all | solution.py:54
  206.4 0.4 convert.2
  206.9 0.2 slice_add_fusion
  207.1 2.4 %gather_fusion = f32[128,3584]{1,0:T(8,128)} fusion(f32[128,3584]{1,0:T(8,128)S(1)} %bitcast.37, s32[1024]{0:T(1024)S(1)} %pad_clamp_fusion), kind=kCustom, calls=%fused_computation | custom fusion | bytes 3670528 | tf_op jit(solution)/shard_map/gather | solution.py:63
  209.5 2.8 %fusion.5 = bf16[16,3584]{1,0:T(8,128)(2,1)} fusion(f32[128,3584]{1,0:T(8,128)} %gather_fusion, f32[16,8]{1,0:T(8,128)S(1)} %copy.23), kind=kLoop, calls=%fused_computation.11 | loop fusion | flops 860160 | bytes 1950208 | tf_op jit(solution)/shard_map/reduce_sum | solution.py:64
  (4 shorter events, 0.1 us)
Async XLA Ops:
  1.7 1.5 copy-start.1
  1.7 1.6 copy-start
  11.1 88.6 %all-to-all-start = ((bf16[16,16,7168]{2,1,0:T(8,128)(2,1)}), bf16[16,16,7168]{2,1,0:T(8,128)(2,1)}, u32[]{:S(2)}, u32[]{:S(2)}) async-start(bf16[16,16,7168]{2,1,0:T(8,128)(2,1)} %bitcast.39), calls=%async_computation | async-start | bytes 7340032 | tf_op jit(solution)/shard_map/all_to_all | solution.py:36
  99.7 49.9 %all-to-all-start.1 = ((bf16[256,2,3584]{2,0,1:T(8,128)(2,1)}), bf16[256,2,3584]{2,0,1:T(8,128)(2,1)}, u32[]{:S(2)}, u32[]{:S(2)}) async-start(bf16[256,2,3584]{2,0,1:T(8,128)(2,1)} %copy.30), calls=%async_computation.1 | async-start | bytes 7340032 | tf_op jit(solution)/shard_map/all_to_all | solution.py:42
  105.2 4.5 %copy-start.3 = (bf16[1,256,7168]{2,1,0:T(8,128)(2,1)S(1)}, bf16[1,256,7168]{2,1,0:T(8,128)(2,1)}, u32[]{:S(2)}) copy-start(bf16[1,256,7168]{2,1,0:T(8,128)(2,1)} %param.10) | copy-start | bytes 11010052
  154.6 10.2 %copy-start.2 = (f32[16,8]{0,1:T(8,128)S(1)}, f32[16,8]{0,1:T(8,128)}, u32[]{:S(2)}) copy-start(f32[16,8]{0,1:T(8,128)} %param.8) | copy-start | bytes 1540
  159.0 47.4 %all-to-all-start.2 = ((bf16[16,16,3584]{2,1,0:T(8,128)(2,1)}), bf16[16,16,3584]{2,1,0:T(8,128)(2,1)S(1)}, u32[]{:S(2)}, u32[]{:S(2)}) async-start(bf16[16,16,3584]{2,1,0:T(8,128)(2,1)} %bitcast.8), calls=%async_computation.2 | async-start | bytes 3670016 | tf_op jit(solution)/shard_map/all_to_all | solution.py:54
where the time goes:
time: 213 us; the launch traced here: 212 us
  waiting for transfers between devices  111 us (52%)
  blocking collectives  41.5 us (19%)
  local copies, waits for them, and re-layouts  18.6 us (9%)
  starting transfers between devices  18.5 us (9%)
  matrix products  13.3 us (6%)
  other arithmetic  9.36 us (4%)
    all_to_all x1, waiting for transfers between devices, body(): lax.all_to_all(jnp.repeat(packed, 2, axis=0), 'expert', split_axis=0, con...  69.4 us
    all_to_all x1, waiting for transfers between devices, body(): lax.all_to_all(half_out.reshape(devices_wide, capacity, -1), 'expert', sp...  41.6 us
    all_gather x1, blocking collectives, body(): shard_piece = lax.all_gather(hidden, 'tensor', axis=1, tiled=True)  36.8 us
    dot_general x2, matrix products, rows_times(): lax.dot_general(rows, weight, (((1,), (1,)), ((), ())), preferred_element...  7.63 us
    all_to_all x1, starting transfers between devices, body(): lax.all_to_all(jnp.repeat(packed, 2, axis=0), 'expert', split_axis=0, con...  7.38 us
    unnamed x10, local copies, waits for them, and re-layouts  6.01 us
    all_to_all x1, local copies, waits for them, and re-layouts, body(): lax.all_to_all(weight_out, 'tensor', split_axis=1, concat_axis=0, tiled=T...  5.95 us
    all_to_all x1, starting transfers between devices, body(): lax.all_to_all(half_out.reshape(devices_wide, capacity, -1), 'expert', sp...  5.63 us
  transfers between devices with their start and end apart: 3, of which 2 were waited for; matrix products, arithmetic and copies ran while one was open for 9% of the time, Pallas kernels for 0%

commit v1 on v0

--- a/solution.py
+++ b/solution.py
@@ -1,7 +1,13 @@
+import functools
+
 import jax
 import jax.numpy as jnp
 from jax import lax
+from jax.experimental import pallas as pl
+from jax.experimental.pallas import tpu as pltpu
 from jax.sharding import PartitionSpec as P
+
+LANES = 128
 
 
 def rows_times(rows, weight):
@@ -10,7 +16,7 @@
     )
 
 
-def body(tokens, expert_ids, route_weights, gate_weight, up_weight, down_weight):
+def sparse_body(tokens, expert_ids, route_weights, gate_weight, up_weight, down_weight):
     devices_wide = lax.axis_size("expert")
     experts = devices_wide // 2
     tok_count = expert_ids.shape[0]
@@ -65,6 +71,397 @@
     return mixed_out.astype(jnp.bfloat16)
 
 
+def fused_kernel(
+    nz, tok_ref, ids_ref, rw_ref, gate_hbm, up_hbm, down_hbm, out_ref,
+    rows_a, rows_b, gate, up, down, part, core_buf, x_buf, y_buf, z_buf, acc,
+    load_sem, row_sem, az_send, ax_send, ay_send, ac_send,
+    core_send, core_recv, x_send, x_recv, y_send, y_recv, z_send, z_recv,
+):
+    me, y = lax.axis_index("expert"), lax.axis_index("tensor")
+    c = lax.rem(me, 2)
+    x = lax.rem(me // 2, 2)
+    z = me // 4
+    oc, ox, oy = 1 - c, 1 - x, 1 - y
+    tok, wide = out_ref.shape
+    half = wide // 2
+    blocks = 2 * nz
+    count = 2 * blocks * tok
+    experts = blocks
+    top = ids_ref.shape[1]
+    rows = (rows_a, rows_b)
+
+    def dev(zz, xx, cc, yy):
+        return ((zz * 2 + xx) * 2 + cc, yy)
+
+    above, below = dev(z + 1, x, c, y), dev(z - 1, x, c, y)
+    dev_x, dev_y, dev_c = dev(z, ox, c, y), dev(z, x, c, oy), dev(z, x, oc, y)
+    has_above, has_below = z < nz - 1, z > 0
+
+    def remote(src, dst, send, recv, to):
+        return pltpu.make_async_remote_copy(
+            src_ref=src, dst_ref=dst, send_sem=send, recv_sem=recv,
+            device_id=to, device_id_type=pl.DeviceIdType.MESH,
+        )
+
+    loads = [
+        pltpu.make_async_copy(src.at[0], dst, load_sem.at[i])
+        for i, (src, dst) in enumerate(((gate_hbm, gate), (up_hbm, up), (down_hbm, down)))
+    ]
+    for load in loads:
+        load.start()
+
+    own = x * nz + z
+    lane = lax.broadcasted_iota(jnp.int32, (tok, LANES), 1)
+    which = lax.rem(lane, experts)
+    spread = jnp.zeros((tok, LANES), jnp.float32)
+    for j in range(top):
+        spread = jnp.where(ids_ref[:, j : j + 1] == which, rw_ref[:, j : j + 1], spread)
+    first = spread.astype(jnp.bfloat16).astype(jnp.float32)
+    rest = spread - first
+    second = rest.astype(jnp.bfloat16).astype(jnp.float32)
+    third = rest - second
+    parts = jnp.where(lane < experts, first, jnp.where(lane < 2 * experts, second, third))
+    parts = jnp.where(lane < 3 * experts, parts, 0.0)
+    rows_a[y, c, own, :, :half] = tok_ref[:, :half]
+    rows_a[y, c, own, :, half:] = parts.astype(jnp.bfloat16)
+    rows_b[y, c, own] = tok_ref[:, half:]
+
+    barrier = pltpu.get_barrier_semaphore()
+    for to in (dev_x, dev_y, dev_c):
+        pl.semaphore_signal(barrier, inc=1, device_id=to, device_id_type=pl.DeviceIdType.MESH)
+
+    @pl.when(has_above)
+    def _():
+        pl.semaphore_signal(barrier, inc=1, device_id=above, device_id_type=pl.DeviceIdType.MESH)
+
+    @pl.when(has_below)
+    def _():
+        pl.semaphore_signal(barrier, inc=1, device_id=below, device_id_type=pl.DeviceIdType.MESH)
+
+    pl.semaphore_wait(barrier, 3 + has_above.astype(jnp.int32) + has_below.astype(jnp.int32))
+
+    def row_copy(h, yy, cc, xx, zz, send, to):
+        at = (yy, cc, xx * nz + zz)
+        return remote(rows[h].at[at], rows[h].at[at], send, row_sem.at[(h,) + at], to)
+
+    def got(h, yy, xx, zz):
+        row_copy(h, yy, c, xx, zz, ac_send.at[h, yy, xx * nz + zz], dev_c).wait_recv()
+
+    def z_copy(h, zz, way):
+        return row_copy(h, y, c, x, zz, az_send.at[way, h, zz], above if way else below)
+
+    def x_copy(h, yy, zz):
+        return row_copy(h, yy, c, x, zz, ax_send.at[h, yy, zz], dev_x)
+
+    def y_copy(h, xx, zz):
+        return row_copy(h, y, c, xx, zz, ay_send.at[h, xx, zz], dev_y)
+
+    def c_copy(h, yy, xx, zz):
+        return row_copy(h, yy, c, xx, zz, ac_send.at[h, yy, xx * nz + zz], dev_c)
+
+    def start_up(h, zz):
+        @pl.when(has_above)
+        def _():
+            z_copy(h, zz, 1).start()
+
+    def start_down(h, zz):
+        @pl.when(has_below)
+        def _():
+            z_copy(h, zz, 0).start()
+
+    def column_sends(zz):
+        x_copy(0, y, zz).start()
+        y_copy(1, x, zz).start()
+        y_copy(0, x, zz).start()
+        x_copy(1, y, zz).start()
+        c_copy(0, y, x, zz).start()
+        c_copy(1, y, x, zz).start()
+
+    def near_first(k):
+        return jnp.where(z < nz // 2, k, nz - 1 - k)
+
+    for h in range(2):
+        start_up(h, z)
+        start_down(h, z)
+    column_sends(z)
+
+    def gather_step(k, carry):
+        zz = near_first(k)
+
+        @pl.when(zz < z)
+        def _():
+            for h in range(2):
+                got(h, y, x, zz)
+                start_up(h, zz)
+
+        @pl.when(zz > z)
+        def _():
+            for h in range(2):
+                got(h, y, x, zz)
+                start_down(h, zz)
+
+        @pl.when(zz != z)
+        def _():
+            column_sends(zz)
+
+        got(0, y, ox, zz)
+        y_copy(0, ox, zz).start()
+        c_copy(0, y, ox, zz).start()
+        got(1, oy, x, zz)
+        x_copy(1, oy, zz).start()
+        c_copy(1, oy, x, zz).start()
+        return carry
+
+    lax.fori_loop(0, nz, gather_step, 0)
+
+    def last_step(k, carry):
+        zz = near_first(k)
+        for h, yy, xx in ((0, oy, x), (1, y, ox), (0, oy, ox), (1, oy, ox)):
+            got(h, yy, xx, zz)
+            c_copy(h, yy, xx, zz).start()
+        return carry
+
+    lax.fori_loop(0, nz, last_step, 0)
+
+    def from_core(k, carry):
+        for h in range(2):
+            for yy in range(2):
+                at = (yy, oc, k)
+                remote(
+                    rows[h].at[at], rows[h].at[at], ac_send.at[h, yy, k], row_sem.at[(h,) + at], dev_c
+                ).wait_recv()
+        return carry
+
+    lax.fori_loop(0, blocks, from_core, 0)
+    loads[0].wait()
+    loads[1].wait()
+
+    contract = (((1,), (1,)), ((), ()))
+    gate_act = up_act = None
+    for yy in range(2):
+        for h in range(2):
+            block = rows[h][yy, :, :, :, :half].reshape(count, half)
+            cols = slice((2 * yy + h) * half, (2 * yy + h + 1) * half)
+            g = lax.dot_general(block, gate[:, cols], contract, preferred_element_type=jnp.float32)
+            u = lax.dot_general(block, up[:, cols], contract, preferred_element_type=jnp.float32)
+            gate_act = g if gate_act is None else gate_act + g
+            up_act = u if up_act is None else up_act + u
+    lanes = lax.broadcasted_iota(jnp.int32, (count, LANES), 1)
+    mine = (lax.rem(lanes, experts) == me // 2) & (lanes < 3 * experts)
+    kept = rows_a[0, :, :, :, half:].reshape(count, LANES).astype(jnp.float32)
+    scale = jnp.sum(jnp.where(mine, kept, 0.0), axis=1, keepdims=True)
+    hidden = (jax.nn.silu(gate_act) * up_act * scale).astype(jnp.bfloat16)
+    loads[2].wait()
+
+    def core_copy(yy, h):
+        return remote(
+            part.at[yy, h, oc], core_buf.at[yy, h], core_send.at[yy, h], core_recv.at[yy, h], dev_c
+        )
+
+    order = ((oy, 0), (oy, 1), (y, 1), (y, 0))
+    for yy, h in order:
+        base = (2 * yy + h) * half
+        piece = 256
+
+        def down_step(k, carry):
+            cols = pl.ds(pl.multiple_of(base + k * piece, 128), piece)
+            got_cols = pl.ds(pl.multiple_of(k * piece, 128), piece)
+            term = jnp.dot(hidden, down[:, cols], preferred_element_type=jnp.float32)
+            part[yy, h, :, :, :, got_cols] = term.astype(jnp.bfloat16).reshape(2, blocks, tok, piece)
+            return carry
+
+        lax.fori_loop(0, half // piece, down_step, 0)
+        core_copy(yy, h).start()
+
+    def far_first(k):
+        return jnp.where(z < nz // 2, nz - 1 - k, k)
+
+    def rx(h, yy, zz):
+        return remote(
+            part.at[yy, h, c, ox * nz + zz], x_buf.at[h, yy, zz], x_send.at[h, yy, zz], x_recv.at[h, yy, zz], dev_x
+        )
+
+    def ry(h, xx, zz):
+        return remote(
+            part.at[oy, h, c, xx * nz + zz], y_buf.at[h, xx, zz], y_send.at[h, xx, zz], y_recv.at[h, xx, zz], dev_y
+        )
+
+    def rz(h, zz, way):
+        return remote(
+            part.at[y, h, c, x * nz + zz], z_buf.at[way, h, zz], z_send.at[way, h, zz], z_recv.at[way, h, zz],
+            above if way else below,
+        )
+
+    wide_f = jnp.float32
+    for yy, h in order:
+        core_copy(yy, h).wait_recv()
+
+        def add_core(k, carry):
+            total = part[yy, h, c, k].astype(wide_f) + core_buf[yy, h, k].astype(wide_f)
+            part[yy, h, c, k] = total.astype(jnp.bfloat16)
+            return carry
+
+        lax.fori_loop(0, blocks, add_core, 0)
+
+        def first_sends(k, carry):
+            zz = far_first(k)
+            if h == 0:
+                ry(0, ox, zz).start()
+                ry(0, x, zz).start()
+            else:
+                rx(1, yy, zz).start()
+            return carry
+
+        if (h == 0) == (yy is oy) or h == 1:
+            lax.fori_loop(0, nz, first_sends, 0)
+
+    def reduce_step(k, carry):
+        zz = far_first(k)
+        ry(0, ox, zz).wait_recv()
+        at = x_of(ox, zz)
+        part[y, 0, c, at] = (part[y, 0, c, at].astype(wide_f) + y_buf[0, ox, zz].astype(wide_f)).astype(jnp.bfloat16)
+        rx(0, y, zz).start()
+        rx(1, oy, zz).wait_recv()
+        at = x_of(x, zz)
+        part[oy, 1, c, at] = (part[oy, 1, c, at].astype(wide_f) + x_buf[1, oy, zz].astype(wide_f)).astype(jnp.bfloat16)
+        ry(1, x, zz).start()
+        return carry
+
+    def x_of(xx, zz):
+        return xx * nz + zz
+
+    lax.fori_loop(0, nz, reduce_step, 0)
+
+    def line_step(k, carry):
+        zz = far_first(k)
+        at = x_of(x, zz)
+        for h in range(2):
+            ry(h, x, zz).wait_recv()
+            rx(h, y, zz).wait_recv()
+            acc[...] = (
+                part[y, h, c, at].astype(wide_f) + y_buf[h, x, zz].astype(wide_f) + x_buf[h, y, zz].astype(wide_f)
+            )
+
+            @pl.when((zz <= z) & has_above)
+            def _():
+                rz(h, zz, 0).wait_recv()
+                acc[...] += z_buf[0, h, zz].astype(wide_f)
+
+            @pl.when((zz >= z) & has_below)
+            def _():
+                rz(h, zz, 1).wait_recv()
+                acc[...] += z_buf[1, h, zz].astype(wide_f)
+
+            @pl.when(zz == z)
+            def _():
+                out_ref[:, h * half : (h + 1) * half] = acc[...].astype(jnp.bfloat16)
+
+            @pl.when(zz != z)
+            def _():
+                part[y, h, c, at] = acc[...].astype(jnp.bfloat16)
+
+            @pl.when(zz < z)
+            def _():
+                rz(h, zz, 0).start()
+
+            @pl.when(zz > z)
+            def _():
+                rz(h, zz, 1).start()
+        return carry
+
+    lax.fori_loop(0, nz, line_step, 0)
+
+    def drain(zz, carry):
+        for h in range(2):
+            @pl.when((zz <= z) & has_above)
+            def _():
+                z_copy(h, zz, 1).wait_send()
+
+            @pl.when((zz >= z) & has_below)
+            def _():
+                z_copy(h, zz, 0).wait_send()
+
+            @pl.when(zz < z)
+            def _():
+                rz(h, zz, 0).wait_send()
+
+            @pl.when(zz > z)
+            def _():
+                rz(h, zz, 1).wait_send()
+
+            for yy in range(2):
+                for xx in range(2):
+                    c_copy(h, yy, xx, zz).wait_send()
+        x_copy(0, y, zz).wait_send()
+        y_copy(1, x, zz).wait_send()
+        rx(0, y, zz).wait_send()
+        ry(1, x, zz).wait_send()
+        for i in range(2):
+            x_copy(1, i, zz).wait_send()
+            y_copy(0, i, zz).wait_send()
+            rx(1, i, zz).wait_send()
+            ry(0, i, zz).wait_send()
+        return carry
+
+    lax.fori_loop(0, nz, drain, 0)
+    for yy in range(2):
+        for h in range(2):
+            core_copy(yy, h).wait_send()
+
+
+def fused_body(tokens, expert_ids, route_weights, gate_weight, up_weight, down_weight):
+    nz = lax.axis_size("expert") // 4
+    tok, wide = tokens.shape
+    half = wide // 2
+    blocks = 2 * nz
+    bf16 = jnp.bfloat16
+    held = gate_weight.shape[1:]
+    vmem = pl.BlockSpec(memory_space=pltpu.VMEM)
+    anywhere = pl.BlockSpec(memory_space=pl.ANY)
+    sems = pltpu.SemaphoreType.DMA
+    return pl.pallas_call(
+        functools.partial(fused_kernel, nz),
+        out_shape=jax.ShapeDtypeStruct((tok, wide), bf16),
+        in_specs=[vmem] * 3 + [anywhere] * 3,
+        out_specs=vmem,
+        scratch_shapes=[
+            pltpu.VMEM((2, 2, blocks, tok, half + LANES), bf16),
+            pltpu.VMEM((2, 2, blocks, tok, half), bf16),
+            pltpu.VMEM(held, bf16),
+            pltpu.VMEM(held, bf16),
+            pltpu.VMEM(held, bf16),
+            pltpu.VMEM((2, 2, 2, blocks, tok, half), bf16),
+            pltpu.VMEM((2, 2, blocks, tok, half), bf16),
+            pltpu.VMEM((2, 2, nz, tok, half), bf16),
+            pltpu.VMEM((2, 2, nz, tok, half), bf16),
+            pltpu.VMEM((2, 2, nz, tok, half), bf16),
+            pltpu.VMEM((tok, half), jnp.float32),
+            sems((3,)),
+            sems((2, 2, 2, blocks)),
+            sems((2, 2, nz)),
+            sems((2, 2, nz)),
+            sems((2, 2, nz)),
+            sems((2, 2, blocks)),
+            sems((2, 2)),
+            sems((2, 2)),
+        ]
+        + [sems((2, 2, nz))] * 6,
+        compiler_params=pltpu.CompilerParams(
+            collective_id=0, has_side_effects=True, vmem_limit_bytes=60 * 2**20
+        ),
+    )(tokens, expert_ids, route_weights, gate_weight, up_weight, down_weight)
+
+
+def body(*args):
+    every = args[1].shape[1] == lax.axis_size("expert") // 2
+    tok, wide = args[0].shape
+    even = lax.axis_size("tensor") == 2 and lax.axis_size("expert") % 8 == 0
+    fits = tok % 16 == 0 and wide % 512 == 0 and 3 * args[1].shape[1] <= LANES
+    if every and even and fits:
+        return fused_body(*args)
+    return sparse_body(*args)
+
+
 def solution(mesh):
     placed = (
         P("expert", "tensor"),

time: 213 us -> 73.1 us (0.34)
  the two profiles are of different devices: /device:TPU:11 before, /device:TPU:0 now
where the time goes in v1:
time: 73.1 us; the launch traced here: 72.9 us
  Pallas kernels  68.6 us (94%)
  local copies, waits for them, and re-layouts  4.26 us (6%)
    pallas_call x1, Pallas kernels, fused_body(): pl.pallas_call(functools.partial(fused_kernel, nz), out_shape=jax.ShapeDt...  68.6 us
    unnamed x3, local copies, waits for them, and re-layouts  4.26 us

profile of v1, /device:TPU:0, one launch (start us, length us, event | category | flops | bytes accessed | tf_op | source)
XLA Modules:
  0.0 72.9 jit_solution(14368370194457793696)
XLA Ops:
  0.0 1.4 %copy.7.ids_ref = s32[16,8]{1,0:T(8,128)} copy(s32[16,8]{0,1:T(8,128)} %param.7) | data formatting | bytes 1024 | tf_op args[1]
  1.4 1.4 %copy.8.rw_ref = f32[16,8]{1,0:T(8,128)} copy(f32[16,8]{0,1:T(8,128)} %param.8) | data formatting | bytes 1024 | tf_op args[2]
  2.7 68.6 %shard_map.64 = bf16[16,3584]{1,0:T(8,128)(2,1)} custom-call(bf16[16,3584]{1,0:T(8,128)(2,1)} %tok_ref.1, s32[16,8]{1,0:T(8,128)} %copy.7.ids_ref, f32[16,8]{1,0:T(8,128)} %copy.8.rw_ref, bf16[1,256,7168]{2,1,0:T(8,128)(2,1)} %gate_hbm.1, bf16[1,256,7168]{2,1,0:T(8,128)(2,1)} %up_hbm.1, bf16[1,256,7168]{2,1,0:T(8,128)(2,1)} %down_hbm.1), custom_call_target="tpu_custom_call" | custom-call | tf_op jit(solution)/shard_map/pallas_call | solution.py:422
  71.3 1.6 %copy.10 = bf16[16,3584]{1,0:T(8,128)(2,1)} copy(bf16[16,3584]{1,0:T(8,128)(2,1)} %shard_map.64) | data formatting | bytes 229376

commit v2 on v0

--- a/solution.py
+++ b/solution.py
@@ -1,7 +1,13 @@
+import functools
+
 import jax
 import jax.numpy as jnp
 from jax import lax
+from jax.experimental import pallas as pl
+from jax.experimental.pallas import tpu as pltpu
 from jax.sharding import PartitionSpec as P
+
+LANES = 128
 
 
 def rows_times(rows, weight):
@@ -10,7 +16,7 @@
     )
 
 
-def body(tokens, expert_ids, route_weights, gate_weight, up_weight, down_weight):
+def sparse_body(tokens, expert_ids, route_weights, gate_weight, up_weight, down_weight):
     devices_wide = lax.axis_size("expert")
     experts = devices_wide // 2
     tok_count = expert_ids.shape[0]
@@ -65,6 +71,358 @@
     return mixed_out.astype(jnp.bfloat16)
 
 
+def fused_kernel(
+    nz, tok_hbm, ids_ref, rw_ref, gate_hbm, up_hbm, down_hbm, out_ref,
+    rows_a, rows_b, gate, up, down, part, core_buf, x_buf, y_buf, z_buf,
+    load_sem, row_sem, az_send, ax_send, ay_send, ac_send,
+    core_send, core_recv, x_send, x_recv, y_send, y_recv, z_send, z_recv,
+):
+    me, y = lax.axis_index("expert"), lax.axis_index("tensor")
+    c = lax.rem(me, 2)
+    x = lax.rem(me // 2, 2)
+    z = me // 4
+    oc, ox, oy = 1 - c, 1 - x, 1 - y
+    tok, wide = out_ref.shape
+    half = wide // 2
+    blocks = 2 * nz
+    count = 2 * blocks * tok
+    experts = blocks
+    top = ids_ref.shape[0]
+    rows = (rows_a, rows_b)
+
+    def dev(zz, xx, cc, yy):
+        return ((zz * 2 + xx) * 2 + cc, yy)
+
+    dev_x, dev_y, dev_c = dev(z, ox, c, y), dev(z, x, c, oy), dev(z, x, oc, y)
+
+    def remote(src, dst, send, recv, to):
+        return pltpu.make_async_remote_copy(
+            src_ref=src, dst_ref=dst, send_sem=send, recv_sem=recv,
+            device_id=to, device_id_type=pl.DeviceIdType.MESH,
+        )
+
+    loads = [
+        pltpu.make_async_copy(src.at[0], dst, load_sem.at[i])
+        for i, (src, dst) in enumerate(((gate_hbm, gate), (up_hbm, up), (down_hbm, down)))
+    ]
+    own = x * nz + z
+    mine_a, mine_b = rows_a.at[y, c, own, :, pl.ds(0, half)], rows_b.at[y, c, own]
+    tok_loads = [
+        pltpu.make_async_copy(tok_hbm.at[:, pl.ds(0, half)], mine_a, load_sem.at[3]),
+        pltpu.make_async_copy(tok_hbm.at[:, pl.ds(half, half)], mine_b, load_sem.at[4]),
+    ]
+    for load in tok_loads + loads:
+        load.start()
+    ids = ids_ref[...].astype(jnp.float32).T
+    weights = rw_ref[...].T
+    lane = lax.broadcasted_iota(jnp.int32, (tok, LANES), 1)
+    which = lax.rem(lane, experts).astype(jnp.float32)
+    spread = jnp.zeros((tok, LANES), jnp.float32)
+    for j in range(top):
+        spread = jnp.where(ids[:, j : j + 1] == which, weights[:, j : j + 1], spread)
+    first = spread.astype(jnp.bfloat16).astype(jnp.float32)
+    rest = spread - first
+    second = rest.astype(jnp.bfloat16).astype(jnp.float32)
+    third = rest - second
+    parts = jnp.where(lane < experts, first, jnp.where(lane < 2 * experts, second, third))
+    parts = jnp.where(lane < 3 * experts, parts, 0.0)
+    rows_a[y, c, own, :, half:] = parts.astype(jnp.bfloat16)
+
+    def other(k):
+        m = nz - 1 - z
+        low = k + (k >= z).astype(jnp.int32)
+        high = nz - 1 - k - (k >= m).astype(jnp.int32)
+        return jnp.where(z < nz // 2, low, high)
+
+    others = [other(k) for k in range(nz - 1)]
+    barrier = pltpu.get_barrier_semaphore()
+    for to in [dev(zz, x, c, y) for zz in others] + [dev_x, dev_y, dev_c]:
+        pl.semaphore_signal(barrier, inc=1, device_id=to, device_id_type=pl.DeviceIdType.MESH)
+    for load in tok_loads:
+        load.wait()
+    pl.semaphore_wait(barrier, nz + 2)
+
+    def row_copy(h, yy, cc, xx, zz, send, to):
+        at = (yy, cc, xx * nz + zz)
+        return remote(rows[h].at[at], rows[h].at[at], send, row_sem.at[(h,) + at], to)
+
+    def z_copy(h, zz):
+        return row_copy(h, y, c, x, z, az_send.at[h, zz], dev(zz, x, c, y))
+
+    def x_copy(h, yy, zz):
+        return row_copy(h, yy, c, x, zz, ax_send.at[h, yy, zz], dev_x)
+
+    def y_copy(h, xx, zz):
+        return row_copy(h, y, c, xx, zz, ay_send.at[h, xx, zz], dev_y)
+
+    def c_copy(h, yy, xx, zz):
+        return row_copy(h, yy, c, xx, zz, ac_send.at[h, yy, xx * nz + zz], dev_c)
+
+    def got(h, yy, xx, zz):
+        c_copy(h, yy, xx, zz).wait_recv()
+
+    def got_forward(h, yy, xx, zz):
+        got(h, yy, xx, zz)
+        c_copy(h, yy, xx, zz).start()
+
+    def column_sends(zz):
+        x_copy(0, y, zz).start()
+        y_copy(1, x, zz).start()
+        y_copy(0, x, zz).start()
+        x_copy(1, y, zz).start()
+        c_copy(0, y, x, zz).start()
+        c_copy(1, y, x, zz).start()
+
+    def second_sends(zz):
+        got(0, y, ox, zz)
+        y_copy(0, ox, zz).start()
+        c_copy(0, y, ox, zz).start()
+        got(1, oy, x, zz)
+        x_copy(1, oy, zz).start()
+        c_copy(1, oy, x, zz).start()
+
+    for zz in others:
+        for h in range(2):
+            z_copy(h, zz).start()
+    column_sends(z)
+    near = [z] + others
+    for k in range(1, nz):
+        for h in range(2):
+            got(h, y, x, near[k])
+        column_sends(near[k])
+        second_sends(near[k - 1])
+    second_sends(near[nz - 1])
+
+    def from_core(h, yy):
+        def step(k, carry):
+            at = (yy, oc, k)
+            remote(rows[h].at[at], rows[h].at[at], ac_send.at[h, yy, k], row_sem.at[(h,) + at], dev_c).wait_recv()
+            return carry
+
+        lax.fori_loop(0, blocks, step, 0)
+
+    contract = (((1,), (1,)), ((), ()))
+
+    def quarter(h, yy):
+        block = rows[h][yy, :, :, :, :half].reshape(count, half)
+        cols = pl.ds(pl.multiple_of((2 * yy + h) * half, LANES), half)
+        g = lax.dot_general(block, gate[:, cols], contract, preferred_element_type=jnp.float32)
+        u = lax.dot_general(block, up[:, cols], contract, preferred_element_type=jnp.float32)
+        return g, u
+
+    for zz in near:
+        got_forward(1, y, ox, zz)
+        got_forward(0, oy, x, zz)
+    loads[0].wait()
+    loads[1].wait()
+    from_core(0, y)
+    gate_0, up_0 = quarter(0, y)
+    for zz in near[: nz // 2]:
+        got_forward(0, oy, ox, zz)
+        got_forward(1, oy, ox, zz)
+    from_core(1, y)
+    gate_1, up_1 = quarter(1, y)
+    for zz in near[nz // 2 :]:
+        got_forward(0, oy, ox, zz)
+        got_forward(1, oy, ox, zz)
+    from_core(0, oy)
+    gate_2, up_2 = quarter(0, oy)
+    from_core(1, oy)
+    gate_3, up_3 = quarter(1, oy)
+    gate_act = gate_0 + gate_1 + gate_2 + gate_3
+    up_act = up_0 + up_1 + up_2 + up_3
+    lanes = lax.broadcasted_iota(jnp.int32, (count, LANES), 1)
+    mine = (lax.rem(lanes, experts) == me // 2) & (lanes < 3 * experts)
+    kept = rows_a[0, :, :, :, half:].reshape(count, LANES).astype(jnp.float32)
+    scale = jnp.sum(jnp.where(mine, kept, 0.0), axis=1, keepdims=True)
+    hidden = (jax.nn.silu(gate_act) * up_act * scale).astype(jnp.bfloat16)
+    loads[2].wait()
+
+    def core_copy(yy, h):
+        return remote(
+            part.at[yy, h, oc], core_buf.at[yy, h], core_send.at[yy, h], core_recv.at[yy, h], dev_c
+        )
+
+    def rx(h, yy, zz):
+        return remote(
+            part.at[yy, h, c, ox * nz + zz], x_buf.at[h, yy, zz], x_send.at[h, yy, zz], x_recv.at[h, yy, zz], dev_x
+        )
+
+    def ry(h, xx, zz):
+        return remote(
+            part.at[oy, h, c, xx * nz + zz], y_buf.at[h, xx, zz], y_send.at[h, xx, zz], y_recv.at[h, xx, zz], dev_y
+        )
+
+    def rz(h, zz, source):
+        return remote(
+            part.at[y, h, c, x * nz + zz], z_buf.at[h, source], z_send.at[h, zz], z_recv.at[h, source],
+            dev(zz, x, c, y),
+        )
+
+    wide_f = jnp.float32
+
+    def project(yy, h):
+        base = (2 * yy + h) * half
+        piece = 256
+
+        def down_step(k, carry):
+            cols = pl.ds(pl.multiple_of(base + k * piece, 128), piece)
+            got_cols = pl.ds(pl.multiple_of(k * piece, 128), piece)
+            term = jnp.dot(hidden, down[:, cols], preferred_element_type=jnp.float32)
+            part[yy, h, :, :, :, got_cols] = term.astype(jnp.bfloat16).reshape(2, blocks, tok, piece)
+            return carry
+
+        lax.fori_loop(0, half // piece, down_step, 0)
+        core_copy(yy, h).start()
+
+    def absorb(yy, h):
+        core_copy(yy, h).wait_recv()
+
+        def add_core(k, carry):
+            total = part[yy, h, c, k].astype(wide_f) + core_buf[yy, h, k].astype(wide_f)
+            part[yy, h, c, k] = total.astype(jnp.bfloat16)
+            return carry
+
+        lax.fori_loop(0, blocks, add_core, 0)
+
+    order = [lax.rem(z + nz - 1 - k, nz) for k in range(nz)]
+
+    def first_y(zz):
+        ry(0, ox, zz).start()
+        ry(0, x, zz).start()
+
+    project(oy, 0)
+    project(oy, 1)
+    absorb(oy, 0)
+    for zz in order[:2]:
+        first_y(zz)
+    project(y, 1)
+    absorb(oy, 1)
+    for zz in order[:2]:
+        rx(1, oy, zz).start()
+    project(y, 0)
+    absorb(y, 1)
+    for zz in order[:2]:
+        rx(1, y, zz).start()
+    absorb(y, 0)
+
+    def turn(zz):
+        at = ox * nz + zz
+        ry(0, ox, zz).wait_recv()
+        part[y, 0, c, at] = (part[y, 0, c, at].astype(wide_f) + y_buf[0, ox, zz].astype(wide_f)).astype(jnp.bfloat16)
+        rx(0, y, zz).start()
+        at = x * nz + zz
+        rx(1, oy, zz).wait_recv()
+        part[oy, 1, c, at] = (part[oy, 1, c, at].astype(wide_f) + x_buf[1, oy, zz].astype(wide_f)).astype(jnp.bfloat16)
+        ry(1, x, zz).start()
+
+    def column_sum(h, zz):
+        ry(h, x, zz).wait_recv()
+        rx(h, y, zz).wait_recv()
+        return (
+            part[y, h, c, x * nz + zz].astype(wide_f) + y_buf[h, x, zz].astype(wide_f) + x_buf[h, y, zz].astype(wide_f)
+        )
+
+    def home(zz):
+        for h in range(2):
+            part[y, h, c, x * nz + zz] = column_sum(h, zz).astype(jnp.bfloat16)
+            rz(h, zz, z).start()
+
+    for k in range(nz):
+        turn(order[k])
+        if k + 2 < nz:
+            first_y(order[k + 2])
+            rx(1, oy, order[k + 2]).start()
+            rx(1, y, order[k + 2]).start()
+        if k > 0:
+            home(order[k - 1])
+    for h in range(2):
+        total = column_sum(h, z)
+        for zz in others:
+            rz(h, z, zz).wait_recv()
+            total = total + z_buf[h, zz].astype(wide_f)
+        out_ref[:, h * half : (h + 1) * half] = total.astype(jnp.bfloat16)
+
+    for zz in others:
+        for h in range(2):
+            z_copy(h, zz).wait_send()
+            rz(h, zz, z).wait_send()
+
+    def drain(zz, carry):
+        for h in range(2):
+            for yy in range(2):
+                for xx in range(2):
+                    c_copy(h, yy, xx, zz).wait_send()
+        x_copy(0, y, zz).wait_send()
+        y_copy(1, x, zz).wait_send()
+        rx(0, y, zz).wait_send()
+        ry(1, x, zz).wait_send()
+        for i in range(2):
+            x_copy(1, i, zz).wait_send()
+            y_copy(0, i, zz).wait_send()
+            rx(1, i, zz).wait_send()
+            ry(0, i, zz).wait_send()
+        return carry
+
+    lax.fori_loop(0, nz, drain, 0)
+    for yy in range(2):
+        for h in range(2):
+            core_copy(yy, h).wait_send()
+
+
+def fused_body(tokens, expert_ids, route_weights, gate_weight, up_weight, down_weight):
+    nz = lax.axis_size("expert") // 4
+    tok, wide = tokens.shape
+    half = wide // 2
+    blocks = 2 * nz
+    bf16 = jnp.bfloat16
+    held = gate_weight.shape[1:]
+    vmem = pl.BlockSpec(memory_space=pltpu.VMEM)
+    anywhere = pl.BlockSpec(memory_space=pl.ANY)
+    sems = pltpu.SemaphoreType.DMA
+    return pl.pallas_call(
+        functools.partial(fused_kernel, nz),
+        out_shape=jax.ShapeDtypeStruct((tok, wide), bf16),
+        in_specs=[anywhere, vmem, vmem] + [anywhere] * 3,
+        out_specs=vmem,
+        scratch_shapes=[
+            pltpu.VMEM((2, 2, blocks, tok, half + LANES), bf16),
+            pltpu.VMEM((2, 2, blocks, tok, half), bf16),
+            pltpu.VMEM(held, bf16),
+            pltpu.VMEM(held, bf16),
+            pltpu.VMEM(held, bf16),
+            pltpu.VMEM((2, 2, 2, blocks, tok, half), bf16),
+            pltpu.VMEM((2, 2, blocks, tok, half), bf16),
+            pltpu.VMEM((2, 2, nz, tok, half), bf16),
+            pltpu.VMEM((2, 2, nz, tok, half), bf16),
+            pltpu.VMEM((2, nz, tok, half), bf16),
+            sems((5,)),
+            sems((2, 2, 2, blocks)),
+            sems((2, nz)),
+            sems((2, 2, nz)),
+            sems((2, 2, nz)),
+            sems((2, 2, blocks)),
+            sems((2, 2)),
+            sems((2, 2)),
+        ]
+        + [sems((2, 2, nz))] * 4
+        + [sems((2, nz))] * 2,
+        compiler_params=pltpu.CompilerParams(
+            collective_id=0, has_side_effects=True, vmem_limit_bytes=60 * 2**20
+        ),
+    )(tokens, expert_ids.T, route_weights.T, gate_weight, up_weight, down_weight)
+
+
+def body(*args):
+    every = args[1].shape[1] == lax.axis_size("expert") // 2
+    tok, wide = args[0].shape
+    even = lax.axis_size("tensor") == 2 and lax.axis_size("expert") % 8 == 0
+    fits = tok % 16 == 0 and wide % 512 == 0 and 3 * args[1].shape[1] <= LANES
+    if every and even and fits:
+        return fused_body(*args)
+    return sparse_body(*args)
+
+
 def solution(mesh):
     placed = (
         P("expert", "tensor"),

time: 213 us -> 61.7 us (0.29)
  the two profiles are of different devices: /device:TPU:11 before, /device:TPU:0 now
where the time goes in v2:
time: 61.7 us; the launch traced here: 61.5 us
  Pallas kernels  60 us (97%)
  local copies, waits for them, and re-layouts  1.55 us (3%)
    pallas_call x1, Pallas kernels, fused_body(): pl.pallas_call(functools.partial(fused_kernel, nz), out_shape=jax.ShapeDt...  60 us
    unnamed x1, local copies, waits for them, and re-layouts  1.55 us

profile of v2, /device:TPU:0, one launch (start us, length us, event | category | flops | bytes accessed | tf_op | source)
XLA Modules:
  0.0 61.5 jit_solution(16083124745317805724)
XLA Ops:
  0.0 60.0 %shard_map.64 = bf16[16,3584]{1,0:T(8,128)(2,1)} custom-call(bf16[16,3584]{1,0:T(8,128)(2,1)} %tok_hbm.1, s32[8,16]{1,0:T(8,128)} %bitcast.2, f32[8,16]{1,0:T(8,128)} %bitcast.3, bf16[1,256,7168]{2,1,0:T(8,128)(2,1)} %gate_hbm.1, bf16[1,256,7168]{2,1,0:T(8,128)(2,1)} %up_hbm.1, bf16[1,256,7168]{2,1,0:T(8,128)(2,1)} %down_hbm.1), custom_call_target="tpu_custom_call" | custom-call | tf_op jit(solution)/shard_map/pallas_call | solution.py:383
  60.0 1.6 %copy.8 = bf16[16,3584]{1,0:T(8,128)(2,1)} copy(bf16[16,3584]{1,0:T(8,128)(2,1)} %shard_map.64) | data formatting | bytes 229376

commit v3 on v2

--- a/solution.py
+++ b/solution.py
@@ -134,7 +134,7 @@
         high = nz - 1 - k - (k >= m).astype(jnp.int32)
         return jnp.where(z < nz // 2, low, high)
 
-    others = [other(k) for k in range(nz - 1)]
+    others = [other(k) for k in reversed(range(nz - 1))]
     barrier = pltpu.get_barrier_semaphore()
     for to in [dev(zz, x, c, y) for zz in others] + [dev_x, dev_y, dev_c]:
         pl.semaphore_signal(barrier, inc=1, device_id=to, device_id_type=pl.DeviceIdType.MESH)
@@ -285,7 +285,7 @@
 
         lax.fori_loop(0, blocks, add_core, 0)
 
-    order = [lax.rem(z + nz - 1 - k, nz) for k in range(nz)]
+    order = others + [z]
 
     def first_y(zz):
         ry(0, ox, zz).start()

time: 61.7 us -> 60.1 us (0.974)
  Pallas kernels: 60 us -> 58.3 us
    pallas_call x1, Pallas kernels: 60 us -> 58.3 us  [fused_body(): pl.pallas_call(functools.partial(fused_kernel, nz), out_shape=jax.ShapeDt...]
where the time goes in v3:
time: 60.1 us; the launch traced here: 59.9 us
  Pallas kernels  58.3 us (97%)
  local copies, waits for them, and re-layouts  1.55 us (3%)
    pallas_call x1, Pallas kernels, fused_body(): pl.pallas_call(functools.partial(fused_kernel, nz), out_shape=jax.ShapeDt...  58.3 us
    unnamed x1, local copies, waits for them, and re-layouts  1.55 us

profile of v3, /device:TPU:0, one launch (start us, length us, event | category | flops | bytes accessed | tf_op | source)
XLA Modules:
  0.0 59.9 jit_solution(1041706043940887479)
XLA Ops:
  0.0 58.3 %shard_map.64 = bf16[16,3584]{1,0:T(8,128)(2,1)} custom-call(bf16[16,3584]{1,0:T(8,128)(2,1)} %tok_hbm.1, s32[8,16]{1,0:T(8,128)} %bitcast.2, f32[8,16]{1,0:T(8,128)} %bitcast.3, bf16[1,256,7168]{2,1,0:T(8,128)(2,1)} %gate_hbm.1, bf16[1,256,7168]{2,1,0:T(8,128)(2,1)} %up_hbm.1, bf16[1,256,7168]{2,1,0:T(8,128)(2,1)} %down_hbm.1), custom_call_target="tpu_custom_call" | custom-call | tf_op jit(solution)/shard_map/pallas_call | solution.py:383
  58.3 1.6 %copy.8 = bf16[16,3584]{1,0:T(8,128)(2,1)} copy(bf16[16,3584]{1,0:T(8,128)(2,1)} %shard_map.64) | data formatting | bytes 229376
